TPU v7x, 32 devices: a whole 2x2x4 slice. The times are simulated.
32 devices in a mesh: dp: 4 (over z), mp: 8 (over y, x, core).
Axes of the slice: x: 2, y: 2, z: 4, core: 2. Of those that a mesh axis runs over, the one named last changes fastest.
Arguments:
- gradients: bfloat16 [4, 2, 768, 2048], P('dp', None, None, 'mp'), may hold values from -4 to 4
- weights: bfloat16 [2, 768, 2048], P(None, None, 'mp'), may hold values from -4 to 4
- projection: float32 [2, 768, 256], replicated, may hold values from -0.21875 to 0.21875
- moment_first: float32 [2, 256, 2048], P(None, 'dp', 'mp'), may hold values from -6 to 6
- moment_second: float32 [2, 256, 2048], P(None, 'dp', 'mp'), may hold values from 0.25 to 4
Outputs:
- new_weights: bfloat16 [2, 768, 2048], P(None, None, 'mp')
- new_first: float32 [2, 256, 2048], P(None, 'dp', 'mp')
- new_second: float32 [2, 256, 2048], P(None, 'dp', 'mp')
- new_bases: float32 [2, 768, 256], replicated
All inputs are finite; a program needn't handle non-finite values.
Results may differ from a plain program's by a relative error of at most 0.0004.
Values may be sent and summed in bfloat16 or wider, within the bound.
A program may use at most 64 MiB of HBM per device.

v0:
```python
import jax
import jax.numpy as jnp
from jax import lax
from jax.sharding import PartitionSpec as P

NS_ITERS = 4


beta_first = 0.5
beta_second = 0.5
adam_eps = 1e-06
learn_rate = 0.1


def newton_schulz(subspace):
    highest = lax.Precision.HIGHEST
    factor = 1.0 / (jnp.sqrt(jnp.sum(subspace * subspace, axis=(1, 2), keepdims=True)) + 1e-06)
    current = subspace * factor
    for sweep in range(NS_ITERS):
        gram = jnp.einsum("ldr,lds->lrs", current, current, precision=highest)
        current = 1.5 * current - 0.5 * jnp.einsum("ldr,lrs->lds", current, gram, precision=highest)
    return current


def back_project(bases_rows, direction_own):
    highest = lax.Precision.HIGHEST
    return jnp.einsum(
        "ldr,lrf->ldf",
        bases_rows,
        lax.all_gather(direction_own, "dp", axis=1, tiled=True),
        precision=highest,
    )


def shards(gradients, weights, projection, moment_first, moment_second):
    highest = lax.Precision.HIGHEST
    local_grad = gradients[0].astype(jnp.float32)
    totals = lax.psum(local_grad, "dp")
    lowrank = jnp.einsum("ldr,ldf->lrf", projection, totals, precision=highest)
    partial_sub = jnp.einsum("ldf,lrf->ldr", totals, lowrank, precision=highest)
    subspace = lax.psum(partial_sub, "mp")
    rank_rows = moment_first.shape[1]
    rank_start = lax.axis_index("dp") * rank_rows
    low_own = lax.dynamic_slice_in_dim(lowrank, rank_start, rank_rows, 1)
    new_first = beta_first * moment_first + (1.0 - beta_first) * low_own
    new_second = beta_second * moment_second + (1.0 - beta_second) * low_own * low_own
    direction_own = new_first / (jnp.sqrt(new_second) + adam_eps)
    width_rows = weights.shape[1] // lax.axis_size("dp")
    row_start = lax.axis_index("dp") * width_rows
    bases_rows = lax.dynamic_slice_in_dim(projection, row_start, width_rows, 1)
    weight_rows = lax.dynamic_slice_in_dim(weights, row_start, width_rows, 1)
    delta_rows = back_project(bases_rows, direction_own)
    updated = (weight_rows.astype(jnp.float32) - learn_rate * delta_rows).astype(jnp.bfloat16)
    new_weights = lax.all_gather(updated, "dp", axis=1, tiled=True)
    new_bases = newton_schulz(subspace)
    return (new_weights, new_first, new_second, new_bases)


def solution(mesh):
    placed = (
        P("dp", None, None, "mp"),
        P(None, None, "mp"),
        P(),
        P(None, "dp", "mp"),
        P(None, "dp", "mp"),
    )
    return jax.shard_map(
        shards,
        mesh=mesh,
        in_specs=placed,
        out_specs=(P(None, None, "mp"), P(None, "dp", "mp"), P(None, "dp", "mp"), P()),
        check_vma=False,
    )
```

profile of v0, /device:TPU:0, one launch (start us, length us, event | category | flops | bytes accessed | tf_op | source)
XLA Modules:
  0.0 174.0 jit_solution(6145538785186923639)
XLA Ops:
  7.2 0.0 copy-start
  7.2 0.0 all-reduce.3.cloned.1.call-start
  7.2 2.5 %bitcast_convert_fusion = f32[2,768,256]{2,1,0:T(8,128)} fusion(bf16[1,2,768,256]{3,2,1,0:T(8,128)(2,1)} %param.5), kind=kLoop, calls=%fused_computation.12 | loop fusion | flops 393216 | bytes 2359296 | tf_op jit(solution)/shard_map/convert_element_type | solution.py:37
  9.7 0.0 all-reduce.3.cloned.1.call-update
  9.8 0.0 all-reduce.5.cloned.1.call-start
  9.8 72.8 %all-reduce.3.cloned.1.call-done = f32[2,768,256]{2,1,0:T(8,128)} async-done(((f32[2,768,256]{2,1,0:T(8,128)}), f32[2,768,256]{2,1,0:T(8,128)}) %all-reduce.3.cloned.1.call-update) | async-done | bytes 1572880 | tf_op jit(solution)/shard_map/psum | solution.py:38
  82.7 0.0 copy-done
  82.7 0.0 copy-start.2
  82.7 4.2 %fusion.11 = f32[2,256,256]{2,1,0:T(8,128)S(1)} fusion(f32[2,768,256]{2,1,0:T(8,128)S(1)} %copy-done, f32[2,768,256]{2,1,0:T(8,128)} %all-reduce.3.cloned.1.call-done), kind=kOutput, calls=%fused_computation.22 | convolution fusion | flops 1207959552 | bytes 3670016 | tf_op jit(solution)/shard_map/ldr,ldf->lrf/dot_general | solution.py:39
  86.9 0.0 copy-done.2
  86.9 2.6 %convolution_bitcast_fusion = f32[2,768,256]{1,2,0:T(8,128)} fusion(f32[2,256,256]{2,1,0:T(8,128)S(1)} %fusion.11, f32[2,768,256]{2,1,0:T(8,128)S(1)} %copy-done.2), kind=kOutput, calls=%fused_computation.5 | convolution fusion | flops 1207959552 | bytes 3670016 | tf_op jit(solution)/shard_map/ldf,lrf->ldr/dot_general | solution.py:40
  89.5 0.0 copy-start.3
  89.5 0.0 copy-start.4
  89.5 0.0 all-reduce.5.cloned.1.call-update
  89.5 0.9 copy-done.3
  90.4 0.1 copy-done.4
  90.5 0.8 add_divide_fusion
  91.2 15.7 %all_gather.6 = f32[2,256,256]{2,1,0:T(8,128)S(1)} all-gather(f32[2,64,256]{2,1,0:T(8,128)S(1)} %get-tuple-element.8), channel_id=1, replica_groups=mesh['dp'=4,'mp'=8] {'dp'}, dimensions={1}, use_global_device_ids=true | all-gather | bytes 655360 | tf_op jit(solution)/shard_map/all_gather | solution.py:30
  106.9 1.5 fusion.4
  108.4 18.3 %all_gather.7 = bf16[2,768,256]{2,1,0:T(8,128)(2,1)} all-gather(bf16[2,192,256]{2,1,0:T(8,128)(2,1)S(1)} %fusion.4), channel_id=1, replica_groups=mesh['dp'=4,'mp'=8] {'dp'}, dimensions={1}, use_global_device_ids=true | all-gather | bytes 983040 | tf_op jit(solution)/shard_map/all_gather | solution.py:54
  126.7 20.9 %all-reduce.5.cloned.1.call-done = f32[2,768,256]{1,2,0:T(8,128)} async-done(((f32[2,768,256]{1,2,0:T(8,128)}), f32[2,768,256]{1,2,0:T(8,128)}) %all-reduce.5.cloned.1.call-update) | async-done | bytes 1572880 | tf_op jit(solution)/shard_map/psum | solution.py:41
  147.6 0.0 copy-start.1
  147.6 1.8 %multiply_reduce_fusion = f32[2]{0:T(128)S(1)} fusion(f32[2,768,256]{1,2,0:T(8,128)} %all-reduce.5.cloned.1.call-done), kind=kLoop, calls=%fused_computation.4 | loop fusion | flops 786430 | bytes 1572872 | tf_op jit(solution)/shard_map/reduce_sum | solution.py:17
  149.4 0.0 copy-done.1
  149.5 1.8 %fusion = f32[2,256,256]{2,1,0:T(8,128)S(1)} fusion(f32[2,768,256]{1,2,0:T(8,128)S(1)} %copy-done.1, f32[2]{0:T(128)S(1)} %add_divide_fusion.1), kind=kOutput, calls=%fused_computation.6 | convolution fusion | flops 1208352768 | bytes 2097160 | tf_op jit(solution)/shard_map/ldr,lds->lrs/dot_general | solution.py:20
  151.2 2.0 %multiply_subtract_fusion.3 = f32[2,768,256]{1,2,0:T(8,128)S(1)} fusion(f32[2,256,256]{2,1,0:T(8,128)S(1)} %fusion, f32[2,768,256]{1,2,0:T(8,128)S(1)} %copy-done.1, f32[2]{0:T(128)S(1)} %add_divide_fusion.1), kind=kOutput, calls=%fused_computation.3 | convolution fusion | flops 1209925632 | bytes 3670024 | tf_op jit(solution)/shard_map/ldr,lrs->lds/dot_general | solution.py:21
  153.2 1.6 fusion.12
  154.9 1.8 %multiply_subtract_fusion.2 = f32[2,768,256]{1,2,0:T(8,128)S(1)} fusion(f32[2,768,256]{1,2,0:T(8,128)S(1)} %multiply_subtract_fusion.3, f32[2,256,256]{2,1,0:T(8,128)S(1)} %fusion.12), kind=kOutput, calls=%fused_computation.2 | convolution fusion | flops 1209139200 | bytes 3670016 | tf_op jit(solution)/shard_map/ldr,lrs->lds/dot_general | solution.py:21
  156.6 1.6 fusion.13
  158.3 1.8 %multiply_subtract_fusion.1 = f32[2,768,256]{1,2,0:T(8,128)S(1)} fusion(f32[2,768,256]{1,2,0:T(8,128)S(1)} %multiply_subtract_fusion.2, f32[2,256,256]{2,1,0:T(8,128)S(1)} %fusion.13), kind=kOutput, calls=%fused_computation.1 | convolution fusion | flops 1209139200 | bytes 3670016 | tf_op jit(solution)/shard_map/ldr,lrs->lds/dot_general | solution.py:21
  160.1 1.6 fusion.14
  161.7 1.8 %multiply_subtract_fusion = f32[2,768,256]{1,2,0:T(8,128)S(1)} fusion(f32[2,768,256]{1,2,0:T(8,128)S(1)} %multiply_subtract_fusion.1, f32[2,256,256]{2,1,0:T(8,128)S(1)} %fusion.14), kind=kOutput, calls=%fused_computation | convolution fusion | flops 1209139200 | bytes 3670016 | tf_op jit(solution)/shard_map/ldr,lrs->lds/dot_general | solution.py:21
  163.5 1.6 copy.18
  165.1 2.1 %copy.31 = bf16[2,768,256]{2,1,0:T(8,128)(2,1)} copy(bf16[2,768,256]{2,1,0:T(8,128)(2,1)} %all_gather.7) | data formatting | bytes 1572864
  (1 shorter events, 0.0 us)
Async XLA Ops:
  7.2 75.5 %copy-start = (f32[2,768,256]{2,1,0:T(8,128)S(1)}, f32[2,768,256]{2,1,0:T(8,128)}, u32[]{:S(2)}) copy-start(f32[2,768,256]{2,1,0:T(8,128)} %param.7) | copy-start | bytes 4718596
  7.2 75.5 %all-reduce.3.cloned.1.call-start = ((), (), s32[]{:S(2)}) async-start(), calls=%async_computation | async-start | bytes 3145728 | tf_op jit(solution)/shard_map/psum | solution.py:38
  9.8 137.8 %all-reduce.5.cloned.1.call-start = ((), (), s32[]{:S(2)}) async-start(), calls=%async_computation.1 | async-start | bytes 3145728 | tf_op jit(solution)/shard_map/psum | solution.py:41
  82.7 4.2 %copy-start.2 = (f32[2,768,256]{2,1,0:T(8,128)S(1)}, f32[2,768,256]{2,1,0:T(8,128)}, u32[]{:S(2)}) copy-start(f32[2,768,256]{2,1,0:T(8,128)} %all-reduce.3.cloned.1.call-done) | copy-start | bytes 4718596
  89.5 0.9 copy-start.3
  89.5 1.0 copy-start.4
  147.6 1.9 %copy-start.1 = (f32[2,768,256]{1,2,0:T(8,128)S(1)}, f32[2,768,256]{1,2,0:T(8,128)}, u32[]{:S(2)}) copy-start(f32[2,768,256]{1,2,0:T(8,128)} %all-reduce.5.cloned.1.call-done) | copy-start | bytes 4718596
Sparse Core Ops, SparseCore 0:
  10.9 71.6 all-reduce.2
  89.7 57.8 all-reduce.4
where the time goes:
time: 174 us
  waiting for transfers between devices  93.7 us (54%)
  blocking collectives  34 us (20%)
  matrix products  22.3 us (13%)
  between operations  14.1 us (8%)
  other arithmetic  5.1 us (3%)
  local copies, waits for them, and re-layouts  4.67 us (3%)
    psum x1, waiting for transfers between devices, shards(): totals = lax.psum(local_grad, 'dp')  72.8 us
    psum x1, waiting for transfers between devices, shards(): subspace = lax.psum(partial_sub, 'mp')  20.9 us
    all_gather x1, blocking collectives, shards(): new_weights = lax.all_gather(updated, 'dp', axis=1, tiled=True)  18.3 us
    all_gather x1, blocking collectives, back_project(): lax.all_gather(direction_own, 'dp', axis=1, tiled=True)  15.7 us
    dot_general x4, matrix products, newton_schulz(): jnp.einsum('ldr,lrs->lds', current, gram, precision=highest)  7.29 us
    dot_general x4, matrix products, newton_schulz(): gram = jnp.einsum('ldr,lds->lrs', current, current, precision=highest)  6.66 us
    unnamed x12, local copies, waits for them, and re-layouts  4.67 us
    dot_general x1, matrix products, shards(): lowrank = jnp.einsum('ldr,ldf->lrf', projection, totals, precision=highest)  4.21 us
  transfers between devices with their start and end apart: 2, of which 2 were waited for; matrix products, arithmetic and copies ran while one was open for 1% of the time, Pallas kernels for 0%

commit v1 on v0

--- a/solution.py
+++ b/solution.py
@@ -1,15 +1,353 @@
+import functools
+
 import jax
 import jax.numpy as jnp
 from jax import lax
+from jax.experimental import pallas as pl
+from jax.experimental.pallas import tpu as pltpu
 from jax.sharding import PartitionSpec as P
 
 NS_ITERS = 4
-
+CORES = 2
+LANES = 128
+SUBLANES = 8
 
 beta_first = 0.5
 beta_second = 0.5
 adam_eps = 1e-06
 learn_rate = 0.1
+
+MESH = pl.DeviceIdType.MESH
+NN = (((1,), (0,)), ((), ()))
+NT = (((1,), (1,)), ((), ()))
+TN = (((0,), (0,)), ((), ()))
+
+
+def split(value):
+    high = value.astype(jnp.bfloat16)
+    low = (value - high.astype(jnp.float32)).astype(jnp.bfloat16)
+    return high, low
+
+
+def product(a, b, dims=NN):
+    dot = functools.partial(lax.dot_general, dimension_numbers=dims, preferred_element_type=jnp.float32)
+    return dot(a[0], b[0]) + (dot(a[0], b[1]) + dot(a[1], b[0]))
+
+
+def step_kernel(
+    n, q, grad, weight, basis, first, second,
+    out_weight, out_first, out_second, out_basis,
+    grad_in, basis_v, basis_t, weight_v, first_v, second_v,
+    low_v, low_in, dir_all, part, plane_in, z_out, z_in, sub,
+    new_weight, new_first, new_second, new_basis,
+    load_sem, store_sem,
+    grad_send, grad_recv, low_send, low_recv, dir_send, dir_recv,
+    plane_send, plane_recv, z_send, z_recv, sub_send, sub_recv, base_send, base_recv,
+):
+    z = lax.axis_index("dp")
+    mp = lax.axis_index("mp")
+    core, plane = lax.rem(mp, CORES), lax.div(mp, CORES)
+    half = n // CORES
+    width = low_v.shape[1]
+    rank_rows = first.shape[1]
+    z_peer = [lax.rem(z + d, n) for d in range(n)]
+    plane_peer = [lax.rem(plane + d, q) for d in range(q)]
+
+    def device(z_at, plane_at, core_at):
+        return (z_at, plane_at * CORES + core_at)
+
+    def remote(src, dst, send, recv, target):
+        return pltpu.make_async_remote_copy(
+            src_ref=src, dst_ref=dst, send_sem=send, recv_sem=recv, device_id=target, device_id_type=MESH
+        )
+
+    def arrived(ref, recv):
+        pltpu.make_async_copy(ref, ref, recv).wait()
+
+    loads = [
+        pltpu.make_async_copy(src, dst, load_sem.at[at])
+        for at, (src, dst) in enumerate(
+            ((basis, basis_v), (first, first_v), (second, second_v), (weight, weight_v))
+        )
+    ]
+    for load in loads:
+        load.start()
+
+    barrier = pltpu.get_barrier_semaphore()
+    for d in range(n):
+        for c in range(CORES):
+            if d + c > 0:
+                target = device(z_peer[d], plane, lax.rem(core + c, CORES))
+                pl.semaphore_signal(barrier, inc=1, device_id=target, device_id_type=MESH)
+    for d in range(1, q):
+        pl.semaphore_signal(barrier, inc=1, device_id=device(z, plane_peer[d], core), device_id_type=MESH)
+    pl.semaphore_wait(barrier, n * CORES - 1 + q - 1)
+
+    grad_sends = []
+    for layer in range(CORES):
+        for s in range(half):
+            owner = core * half + s
+            src = grad.at[0, layer, :, pl.ds(s * width, width)]
+            own = jnp.logical_and(owner == z, core == layer)
+            send = remote(
+                src, grad_in.at[z], grad_send.at[layer, s], grad_recv.at[z], device(owner, plane, layer)
+            )
+
+            @pl.when(own)
+            def _(src=src):
+                pltpu.make_async_copy(src, grad_in.at[z], grad_recv.at[z]).start()
+
+            @pl.when(jnp.logical_not(own))
+            def _(send=send):
+                send.start()
+
+            grad_sends.append((own, send))
+
+    loads[0].wait()
+    t_high, t_low = split(basis_v[core].T)
+    basis_t[0] = t_high
+    basis_t[1] = t_low
+
+    for d in range(n):
+        arrived(grad_in.at[z_peer[d]], grad_recv.at[z_peer[d]])
+    total = grad_in[0].astype(jnp.float32)
+    for r in range(1, n):
+        total = total + grad_in[r].astype(jnp.float32)
+    total = split(total)
+    low = product((basis_t[0], basis_t[1]), total)
+    low_v[...] = low
+
+    column_core, column_slot = lax.div(z, half), lax.rem(z, half)
+    low_sends = []
+    for d in range(n):
+        src = low_v.at[pl.ds(pl.multiple_of(z_peer[d] * rank_rows, SUBLANES), rank_rows), :]
+        dst = low_in.at[core, column_slot]
+        recv = low_recv.at[core, column_slot]
+        send = remote(src, dst, low_send.at[d], recv, device(z_peer[d], plane, column_core))
+        if d > 0:
+            send.start()
+            low_sends.append((None, send))
+        else:
+            own = column_core == core
+
+            @pl.when(own)
+            def _(src=src, dst=dst, recv=recv):
+                pltpu.make_async_copy(src, dst, recv).start()
+
+            @pl.when(jnp.logical_not(own))
+            def _(send=send):
+                send.start()
+
+            low_sends.append((own, send))
+
+    part[...] = product(total, split(low), NT).reshape(part.shape)
+    plain_sends = []
+    for e in list(range(1, n)) + [0]:
+        for d in range(1, q):
+            send = remote(
+                part.at[plane_peer[d], z_peer[e]], plane_in.at[plane, z_peer[e]],
+                plane_send.at[d, e], plane_recv.at[plane, z_peer[e]], device(z, plane_peer[d], core),
+            )
+            send.start()
+            plain_sends.append(send)
+
+    for layer in range(CORES):
+        for s in range(half):
+            arrived(low_in.at[layer, s], low_recv.at[layer, s])
+    loads[1].wait()
+    loads[2].wait()
+    for layer in range(CORES):
+        for s in range(half):
+            columns = pl.ds(s * width, width)
+            mine = low_in[layer, s]
+            moved = beta_first * first_v[layer, :, columns] + (1.0 - beta_first) * mine
+            spread = beta_second * second_v[layer, :, columns] + (1.0 - beta_second) * mine * mine
+            new_first[layer, :, columns] = moved
+            new_second[layer, :, columns] = spread
+            dir_all[z, layer, :, columns] = moved / (jnp.sqrt(spread) + adam_eps)
+    for d in range(1, n):
+        send = remote(
+            dir_all.at[z], dir_all.at[z], dir_send.at[d], dir_recv.at[z], device(z_peer[d], plane, core)
+        )
+        send.start()
+        plain_sends.append(send)
+    stores = [
+        pltpu.make_async_copy(new_first, out_first, store_sem.at[0]),
+        pltpu.make_async_copy(new_second, out_second, store_sem.at[1]),
+    ]
+    for store in stores:
+        store.start()
+
+    def plane_sum(e):
+        for d in range(1, q):
+            arrived(plane_in.at[plane_peer[d], z_peer[e]], plane_recv.at[plane_peer[d], z_peer[e]])
+        value = part[plane, z_peer[e]]
+        for d in range(1, q):
+            value = value + plane_in[plane_peer[d], z_peer[e]]
+        return value
+
+    for e in range(1, n):
+        z_out[e] = plane_sum(e)
+        send = remote(
+            z_out.at[e], z_in.at[z], z_send.at[e], z_recv.at[z], device(z_peer[e], plane, core)
+        )
+        send.start()
+        plain_sends.append(send)
+    value = plane_sum(0)
+    for e in range(1, n):
+        arrived(z_in.at[z_peer[e]], z_recv.at[z_peer[e]])
+    for e in range(1, n):
+        value = value + z_in[z_peer[e]]
+    sub[plane, z] = value
+
+    def spread_plane(e):
+        for d in range(1, q):
+            block = sub.at[plane, z_peer[e]]
+            send = remote(
+                block, block, sub_send.at[d, e], sub_recv.at[plane, z_peer[e]], device(z, plane_peer[d], core)
+            )
+            send.start()
+            plain_sends.append(send)
+
+    for e in range(1, n):
+        block = sub.at[plane, z]
+        send = remote(block, block, sub_send.at[0, e], sub_recv.at[plane, z], device(z_peer[e], plane, core))
+        send.start()
+        plain_sends.append(send)
+    spread_plane(0)
+
+    for d in range(1, n):
+        arrived(dir_all.at[z_peer[d]], dir_recv.at[z_peer[d]])
+    loads[3].wait()
+
+    def update(layer):
+        direction = dir_all[:, layer].reshape(n * rank_rows, dir_all.shape[3])
+        delta = product(split(basis_v[layer]), split(direction))
+        new_weight[layer] = (weight_v[layer].astype(jnp.float32) - learn_rate * delta).astype(jnp.bfloat16)
+
+    update(0)
+    for e in range(1, n):
+        arrived(sub.at[plane, z_peer[e]], sub_recv.at[plane, z_peer[e]])
+        spread_plane(e)
+    update(1)
+    store = pltpu.make_async_copy(new_weight, out_weight, store_sem.at[2])
+    store.start()
+    stores.append(store)
+
+    for e in range(n):
+        for d in range(1, q):
+            arrived(sub.at[plane_peer[d], z_peer[e]], sub_recv.at[plane_peer[d], z_peer[e]])
+
+    depth, rank = new_basis.shape
+    current = sub[...].reshape(depth, rank)
+    current = current * (1.0 / (jnp.sqrt(jnp.sum(current * current)) + 1e-06))
+    start = split(current)
+    gram = product(start, start, TN)
+    rows = lax.broadcasted_iota(jnp.int32, (rank, rank), 0)
+    columns = lax.broadcasted_iota(jnp.int32, (rank, rank), 1)
+    scaled_eye = jnp.where(rows == columns, 1.5, 0.0)
+    chain = None
+    for sweep in range(NS_ITERS):
+        factor = scaled_eye - 0.5 * gram
+        pieces = split(factor)
+        chain = factor if chain is None else product(split(chain), pieces)
+        if sweep < NS_ITERS - 1:
+            gram = product(pieces, split(product(split(gram), pieces)))
+    chain = split(chain)
+    chunk = depth // q
+    base_copies = []
+    for at in range(q):
+        span = pl.ds(at * chunk, chunk)
+        lines = slice(at * chunk, (at + 1) * chunk)
+        new_basis[span, :] = product((start[0][lines], start[1][lines]), chain)
+        send = remote(
+            new_basis.at[span, :], out_basis.at[core, span, :], base_send.at[at], base_recv.at[at],
+            device(z, plane, 1 - core),
+        )
+        send.start()
+        plain_sends.append(send)
+        store = pltpu.make_async_copy(new_basis.at[span, :], out_basis.at[core, span, :], store_sem.at[3 + at])
+        store.start()
+        stores.append(store)
+
+    for own, send in grad_sends + low_sends:
+        if own is None:
+            send.wait_send()
+        else:
+            @pl.when(jnp.logical_not(own))
+            def _(send=send):
+                send.wait_send()
+    for send in plain_sends:
+        send.wait_send()
+    for at in range(q):
+        block = out_basis.at[1 - core, pl.ds(at * chunk, chunk), :]
+        arrived(block, base_recv.at[at])
+    for store in stores:
+        store.wait()
+
+
+def fused_step(gradients, weights, projection, moment_first, moment_second):
+    n = lax.axis_size("dp")
+    q = lax.axis_size("mp") // CORES
+    layers, depth, columns = weights.shape
+    rank = projection.shape[2]
+    rank_rows = moment_first.shape[1]
+    half = n // CORES
+    width = columns // half
+    piece = depth // (q * n)
+    f32, bf16 = jnp.float32, jnp.bfloat16
+    dma = pltpu.SemaphoreType.DMA
+    anywhere = pl.BlockSpec(memory_space=pl.ANY)
+    outs = pl.pallas_call(
+        functools.partial(step_kernel, n, q),
+        name="galore_step",
+        out_shape=(
+            jax.ShapeDtypeStruct(weights.shape, bf16),
+            jax.ShapeDtypeStruct(moment_first.shape, f32),
+            jax.ShapeDtypeStruct(moment_second.shape, f32),
+            jax.ShapeDtypeStruct(projection.shape, f32),
+        ),
+        in_specs=[anywhere] * 5,
+        out_specs=(anywhere,) * 4,
+        scratch_shapes=[
+            pltpu.VMEM((n, depth, width), bf16),
+            pltpu.VMEM(projection.shape, f32),
+            pltpu.VMEM((2, rank, depth), bf16),
+            pltpu.VMEM(weights.shape, bf16),
+            pltpu.VMEM(moment_first.shape, f32),
+            pltpu.VMEM(moment_second.shape, f32),
+            pltpu.VMEM((rank, width), f32),
+            pltpu.VMEM((CORES, half, rank_rows, width), f32),
+            pltpu.VMEM((n, layers, rank_rows, columns), f32),
+            pltpu.VMEM((q, n, piece, rank), f32),
+            pltpu.VMEM((q, n, piece, rank), f32),
+            pltpu.VMEM((n, piece, rank), f32),
+            pltpu.VMEM((n, piece, rank), f32),
+            pltpu.VMEM((q, n, piece, rank), f32),
+            pltpu.VMEM(weights.shape, bf16),
+            pltpu.VMEM(moment_first.shape, f32),
+            pltpu.VMEM(moment_second.shape, f32),
+            pltpu.VMEM((depth, rank), f32),
+            dma((4,)),
+            dma((3 + q,)),
+            dma((CORES, half)),
+            dma((n,)),
+            dma((n,)),
+            dma((CORES, half)),
+            dma((n,)),
+            dma((n,)),
+            dma((q, n)),
+            dma((q, n)),
+            dma((n,)),
+            dma((n,)),
+            dma((q, n)),
+            dma((q, n)),
+            dma((q,)),
+            dma((q,)),
+        ],
+        compiler_params=pltpu.CompilerParams(collective_id=0, has_side_effects=True),
+    )(gradients, weights, projection, moment_first, moment_second)
+    return tuple(outs)
 
 
 def newton_schulz(subspace):
@@ -32,7 +370,7 @@
     )
 
 
-def shards(gradients, weights, projection, moment_first, moment_second):
+def plain_step(gradients, weights, projection, moment_first, moment_second):
     highest = lax.Precision.HIGHEST
     local_grad = gradients[0].astype(jnp.float32)
     totals = lax.psum(local_grad, "dp")
@@ -56,6 +394,23 @@
     return (new_weights, new_first, new_second, new_bases)
 
 
+def shards(gradients, weights, projection, moment_first, moment_second):
+    n = lax.axis_size("dp")
+    q = lax.axis_size("mp") // CORES
+    layers, depth, columns = weights.shape
+    rank_rows = moment_first.shape[1]
+    whole_tiles = (
+        layers == CORES
+        and gradients.shape[0] == 1
+        and n % CORES == 0
+        and columns % (n // CORES * LANES) == 0
+        and depth % (q * n * SUBLANES) == 0
+        and rank_rows % SUBLANES == 0
+    )
+    step = fused_step if whole_tiles else plain_step
+    return step(gradients, weights, projection, moment_first, moment_second)
+
+
 def solution(mesh):
     placed = (
         P("dp", None, None, "mp"),

time: 174 us -> 71.6 us (0.41)
  waiting for transfers between devices: 93.7 us -> 0 us
  Pallas kernels: 0 us -> 65.2 us
  blocking collectives: 34 us -> 0 us
  matrix products: 22.3 us -> 0 us
  between operations: 14.1 us -> 0.66 us
  other arithmetic: 5.1 us -> 0 us
    psum x2 -> x0, waiting for transfers between devices: 93.7 us -> none  [the longest x1 72.8 us: shards(): totals = lax.psum(local_grad, 'dp')]
    pallas_call x0 -> x1, Pallas kernels: none -> 65.2 us  [fused_step(): pl.pallas_call(functools.partial(step_kernel, n, q), name='galore_step',...]
    all_gather x2 -> x0, blocking collectives: 34 us -> none  [the longest x1 18.3 us: shards(): new_weights = lax.all_gather(updated, 'dp', axis=1, tiled=True)]
    dot_general x11 -> x0, matrix products: 22.3 us -> none  [the longest x4 7.29 us: newton_schulz(): jnp.einsum('ldr,lrs->lds', current, gram, precision=highest)]
    convert_element_type x1 -> x0, other arithmetic: 2.51 us -> none  [shards(): local_grad = gradients[0].astype(jnp.float32)]
    reduce_sum x1 -> x0, other arithmetic: 1.83 us -> none  [newton_schulz(): jnp.sum(subspace * subspace, axis=(1, 2), keepdims=True)]
    unnamed x12 -> x8, local copies, waits for them, and re-layouts: 4.67 us -> 5.56 us
  transfers between devices with their start and end apart: 2 -> 0, of which waited for: 2 -> 0; matrix products, arithmetic and copies ran while one was open for 1% -> 0% of each run, Pallas kernels for 0% -> 0%
where the time goes in v1:
time: 71.6 us; the launch traced here: 71.4 us
  Pallas kernels  65.2 us (91%)
  local copies, waits for them, and re-layouts  5.56 us (8%)
    pallas_call x1, Pallas kernels, fused_step(): pl.pallas_call(functools.partial(step_kernel, n, q), name='galore_step',...  65.2 us
    unnamed x8, local copies, waits for them, and re-layouts  5.56 us

profile of v1, /device:TPU:0, one launch (start us, length us, event | category | flops | bytes accessed | tf_op | source)
XLA Modules:
  0.0 71.4 jit_solution(17988005615612819261)
XLA Ops:
  0.6 65.2 %galore_step.1 = (bf16[2,768,256]{2,1,0:T(8,128)(2,1)}, f32[2,64,256]{2,1,0:T(8,128)}, f32[2,64,256]{2,1,0:T(8,128)}, f32[2,768,256]{2,1,0:T(8,128)}) custom-call(bf16[1,2,768,256]{3,2,1,0:T(8,128)(2,1)} %grad.1, bf16[2,768,256]{2,1,0:T(8,128)(2,1)} %weight.1, f32[2,768,256]{2,1,0:T(8,128)} %basis.1, f32[2,64,256]{2,1,0:T(8,128)} %first.1, f32[2,64,256]{2,1,0:T(8,128)} %second.1), custom_call_target="tpu_custom_call" | custom-call | tf_op jit(solution)/shard_map/galore_step/pallas_call | solution.py:301
  65.8 0.0 copy-start.1
  65.8 0.0 copy-start
  65.8 2.2 %copy.13 = bf16[2,768,256]{2,1,0:T(8,128)(2,1)} copy(bf16[2,768,256]{2,1,0:T(8,128)(2,1)} %get-tuple-element.8) | data formatting | bytes 1572864
  68.0 1.6 %copy.14 = f32[2,64,256]{2,1,0:T(8,128)} copy(f32[2,64,256]{2,1,0:T(8,128)} %get-tuple-element.9) | data formatting | bytes 262144
  69.6 0.0 copy-done.1
  69.6 0.7 copy.15
  70.2 0.0 copy-done
  70.2 1.1 %copy.16 = f32[2,768,256]{2,1,0:T(8,128)} copy(f32[2,768,256]{2,1,0:T(8,128)S(1)} %copy-done) | data formatting | bytes 3145728
Async XLA Ops:
  65.8 3.8 %copy-start.1 = (f32[2,64,256]{2,1,0:T(8,128)S(1)}, f32[2,64,256]{2,1,0:T(8,128)}, u32[]{:S(2)}) copy-start(f32[2,64,256]{2,1,0:T(8,128)} %get-tuple-element.10) | copy-start | bytes 393220
  65.8 4.4 %copy-start = (f32[2,768,256]{2,1,0:T(8,128)S(1)}, f32[2,768,256]{2,1,0:T(8,128)}, u32[]{:S(2)}) copy-start(f32[2,768,256]{2,1,0:T(8,128)} %get-tuple-element.11) | copy-start | bytes 4718596

commit v2 on v1

--- a/solution.py
+++ b/solution.py
@@ -40,7 +40,7 @@
     grad_in, basis_v, basis_t, weight_v, first_v, second_v,
     low_v, low_in, dir_all, part, plane_in, z_out, z_in, sub,
     new_weight, new_first, new_second, new_basis,
-    load_sem, store_sem,
+    load_sem, store_sem, weight_sem,
     grad_send, grad_recv, low_send, low_recv, dir_send, dir_recv,
     plane_send, plane_recv, z_send, z_recv, sub_send, sub_recv, base_send, base_recv,
 ):
@@ -165,12 +165,6 @@
             new_first[layer, :, columns] = moved
             new_second[layer, :, columns] = spread
             dir_all[z, layer, :, columns] = moved / (jnp.sqrt(spread) + adam_eps)
-    for d in range(1, n):
-        send = remote(
-            dir_all.at[z], dir_all.at[z], dir_send.at[d], dir_recv.at[z], device(z_peer[d], plane, core)
-        )
-        send.start()
-        plain_sends.append(send)
     stores = [
         pltpu.make_async_copy(new_first, out_first, store_sem.at[0]),
         pltpu.make_async_copy(new_second, out_second, store_sem.at[1]),
@@ -217,22 +211,14 @@
     spread_plane(0)
 
     for d in range(1, n):
-        arrived(dir_all.at[z_peer[d]], dir_recv.at[z_peer[d]])
-    loads[3].wait()
-
-    def update(layer):
-        direction = dir_all[:, layer].reshape(n * rank_rows, dir_all.shape[3])
-        delta = product(split(basis_v[layer]), split(direction))
-        new_weight[layer] = (weight_v[layer].astype(jnp.float32) - learn_rate * delta).astype(jnp.bfloat16)
-
-    update(0)
+        send = remote(
+            dir_all.at[z], dir_all.at[z], dir_send.at[d], dir_recv.at[z], device(z_peer[d], plane, core)
+        )
+        send.start()
+        plain_sends.append(send)
     for e in range(1, n):
         arrived(sub.at[plane, z_peer[e]], sub_recv.at[plane, z_peer[e]])
         spread_plane(e)
-    update(1)
-    store = pltpu.make_async_copy(new_weight, out_weight, store_sem.at[2])
-    store.start()
-    stores.append(store)
 
     for e in range(n):
         for d in range(1, q):
@@ -270,6 +256,17 @@
         store.start()
         stores.append(store)
 
+    for d in range(1, n):
+        arrived(dir_all.at[z_peer[d]], dir_recv.at[z_peer[d]])
+    loads[3].wait()
+    for layer in range(CORES):
+        direction = dir_all[:, layer].reshape(n * rank_rows, dir_all.shape[3])
+        delta = product(split(basis_v[layer]), split(direction))
+        new_weight[layer] = (weight_v[layer].astype(jnp.float32) - learn_rate * delta).astype(jnp.bfloat16)
+        store = pltpu.make_async_copy(new_weight.at[layer], out_weight.at[layer], weight_sem.at[layer])
+        store.start()
+        stores.append(store)
+
     for own, send in grad_sends + low_sends:
         if own is None:
             send.wait_send()
@@ -284,6 +281,42 @@
         arrived(block, base_recv.at[at])
     for store in stores:
         store.wait()
+
+
+def pass_kernel(weight, first, second, basis, out_weight, out_first, out_second, out_basis,
+                weight_v, first_v, second_v, basis_v, read_sem, write_sem):
+    layers = basis.shape[0]
+    depth = basis.shape[1] // 2
+    parts = []
+    for layer in range(layers):
+        for at in range(2):
+            span = pl.ds(at * depth, depth)
+            parts.append(tuple(ref.at[layer, span, :] for ref in (basis, basis_v, out_basis)))
+        for refs in ((weight, weight_v, out_weight), (first, first_v, out_first), (second, second_v, out_second)):
+            parts.append(tuple(ref.at[layer] for ref in refs))
+    reads = [pltpu.make_async_copy(src, mid, read_sem.at[at]) for at, (src, mid, _) in enumerate(parts)]
+    writes = [pltpu.make_async_copy(mid, dst, write_sem.at[at]) for at, (_, mid, dst) in enumerate(parts)]
+    for read in reads:
+        read.start()
+    for read, write in zip(reads, writes):
+        read.wait()
+        write.start()
+    for write in writes:
+        write.wait()
+
+
+def pass_on(*arrays):
+    anywhere = pl.BlockSpec(memory_space=pl.ANY)
+    count = 5 * arrays[3].shape[0]
+    return pl.pallas_call(
+        pass_kernel,
+        name="pass_on",
+        out_shape=tuple(jax.ShapeDtypeStruct(a.shape, a.dtype) for a in arrays),
+        in_specs=[anywhere] * 4,
+        out_specs=(anywhere,) * 4,
+        scratch_shapes=[pltpu.VMEM(a.shape, a.dtype) for a in arrays]
+        + [pltpu.SemaphoreType.DMA((count,)), pltpu.SemaphoreType.DMA((count,))],
+    )(*arrays)
 
 
 def fused_step(gradients, weights, projection, moment_first, moment_second):
@@ -330,6 +363,7 @@
             pltpu.VMEM((depth, rank), f32),
             dma((4,)),
             dma((3 + q,)),
+            dma((CORES,)),
             dma((CORES, half)),
             dma((n,)),
             dma((n,)),
@@ -347,7 +381,7 @@
         ],
         compiler_params=pltpu.CompilerParams(collective_id=0, has_side_effects=True),
     )(gradients, weights, projection, moment_first, moment_second)
-    return tuple(outs)
+    return pass_on(*outs)
 
 
 def newton_schulz(subspace):

time: 71.6 us -> 63.7 us (0.89)
  the two profiles are of different devices: /device:TPU:0 before, /device:TPU:15 now
where the time goes in v2:
time: 63.7 us; the launch traced here: 63.6 us
  Pallas kernels  62.9 us (99%)
  between operations  0.64 us (1%)
    pallas_call x1, Pallas kernels, fused_step(): pl.pallas_call(functools.partial(step_kernel, n, q), name='galore_step',...  60.3 us
    pallas_call x1, Pallas kernels, pass_on(): pl.pallas_call(pass_kernel, name='pass_on', out_shape=tuple((jax.ShapeDty...  2.64 us

profile of v2, /device:TPU:15, one launch (start us, length us, event | category | flops | bytes accessed | tf_op | source)
XLA Modules:
  0.0 63.6 jit_solution(6280915207555109744)
XLA Ops:
  0.6 60.3 %galore_step.1 = (bf16[2,768,256]{2,1,0:T(8,128)(2,1)}, f32[2,64,256]{2,1,0:T(8,128)}, f32[2,64,256]{2,1,0:T(8,128)}, f32[2,768,256]{2,1,0:T(8,128)}) custom-call(bf16[1,2,768,256]{3,2,1,0:T(8,128)(2,1)} %grad.1, bf16[2,768,256]{2,1,0:T(8,128)(2,1)} %weight.1, f32[2,768,256]{2,1,0:T(8,128)} %basis.1, f32[2,64,256]{2,1,0:T(8,128)} %first.1, f32[2,64,256]{2,1,0:T(8,128)} %second.1), custom_call_target="tpu_custom_call" | custom-call | tf_op jit(solution)/shard_map/galore_step/pallas_call | solution.py:334
  60.9 2.6 %pass_on.1 = (bf16[2,768,256]{2,1,0:T(8,128)(2,1)}, f32[2,64,256]{2,1,0:T(8,128)}, f32[2,64,256]{2,1,0:T(8,128)}, f32[2,768,256]{2,1,0:T(8,128)}) custom-call(bf16[2,768,256]{2,1,0:T(8,128)(2,1)} %get-tuple-element.8.weight, f32[2,64,256]{2,1,0:T(8,128)} %get-tuple-element.9.first, f32[2,64,256]{2,1,0:T(8,128)} %get-tuple-element.10.second, ...), custom_call_target="tpu_custom_call" | custom-call | tf_op jit(solution)/shard_map/pass_on/pallas_call | solution.py:311
